TPU v7x, 256 devices: a whole 4x4x8 slice. The times are simulated.
256 devices in a mesh: seq: 64 (over x, z, core), head: 4 (over y).
Axes of the slice: x: 4, y: 4, z: 8, core: 2. Of those that a mesh axis runs over, the one named last changes fastest.
Arguments:
- face_rows: bfloat16 [16384, 1024], P('seq', 'head'), may hold values from -400 to 400
- norm_gain: float32 [1024], replicated, may hold values from 0.25 to 1.75
- w_qkv: bfloat16 [1024, 3, 1024], P(None, None, 'head'), may hold values from -1.875 to 1.875
- w_out: bfloat16 [1024, 1024], P('head'), may hold values from -0.1875 to 0.1875
- segments: int32 [16384], P('seq'), may hold values from 0 to 3, never falling along the last dimension, each value on 1 to 8192 neighbouring positions
Outputs:
- mixed: bfloat16 [16384, 1024], P('seq', 'head')
All inputs are finite; a program needn't handle non-finite values.
Results may differ from a plain program's by a relative error of at most 0.004.
The roundings to bfloat16 on the way count: a program that leaves them out, or rounds other values in their place, can miss the bound.
Values may be sent and summed in bfloat16 or wider, within the bound.
A program may use at most 128 MiB of HBM per device.

v0:
```python
import functools
import math
import jax
import jax.numpy as jnp
from jax import lax
from jax.sharding import PartitionSpec as P

HD = 128
epsilon = 1e-05
masked_score = -1e30


def attend_piece(states, piece, start, groups, head_count):
    keys_vals, key_segments = piece
    key_count = keys_vals.shape[1]
    head_size = keys_vals.shape[2] // head_count
    key_rows = keys_vals[0].reshape(key_count, head_count, head_size)
    value_rows = keys_vals[1].reshape(key_count, head_count, head_size)
    key_positions = lax.iota(jnp.int32, key_count)
    key_seg = key_segments[0].astype(jnp.float32)
    updated = []
    for group, state in zip(groups, states):
        group_queries, query_positions, query_seg = group

        def update(
            current,
            group_queries=group_queries,
            query_positions=query_positions,
            query_seg=query_seg,
        ):
            run_max, run_total, run_acc = current
            scores = jnp.einsum(
                "qhd,khd->hqk", group_queries, key_rows, preferred_element_type=jnp.float32
            )
            allowed = (key_positions[None, :] <= query_positions[:, None]) & (
                key_seg[None, :] == query_seg[:, None]
            )
            scores = jnp.where(allowed[None], scores, masked_score)
            new_max = jnp.maximum(run_max, jnp.max(scores, axis=2))
            factor = jnp.exp(run_max - new_max)
            weights = jnp.where(allowed[None], jnp.exp(scores - new_max[:, :, None]), 0.0)
            new_total = jnp.sum(weights, axis=2)
            new_acc = jnp.einsum(
                "hqk,khd->hqd",
                weights.astype(jnp.bfloat16),
                value_rows,
                preferred_element_type=jnp.float32,
            )
            return (new_max, new_total, new_acc)

        needed = (start <= jnp.max(query_positions)) & (
            key_seg[key_count - 1] >= jnp.min(query_seg)
        )
        updated.append(lax.cond(needed, update, lambda current: current, state))
    return tuple(updated)


def finish(state, width):
    run_max, run_total, run_acc = state
    result = run_acc / run_total[:, :, None]
    return jnp.transpose(result, (1, 0, 2)).reshape(result.shape[1], width).astype(jnp.bfloat16)


def per_device(face_rows, norm_gain, w_qkv, w_out, segments):
    whole = lax.all_gather(face_rows, "head", axis=1, tiled=True)
    row_count, model_width = whole.shape
    width = w_qkv.shape[2]
    head_count = width // HD
    half = row_count // 2
    values32 = whole.astype(jnp.float32)
    normed = (
        values32
        * lax.rsqrt(jnp.mean(values32 * values32, axis=1, keepdims=True) + epsilon)
        * norm_gain
    ).astype(jnp.bfloat16)
    projected = jnp.dot(
        normed, w_qkv.reshape(model_width, 3 * width), preferred_element_type=jnp.float32
    )
    queries = (projected[:, :width] * (1.0 / math.sqrt(HD))).astype(jnp.bfloat16)
    keys_vals = jnp.stack([projected[:, width : 2 * width], projected[:, 2 * width :]]).astype(
        jnp.bfloat16
    )
    shard_index = lax.axis_index("seq")
    positions = shard_index * row_count + lax.iota(jnp.int32, row_count)
    seg_values = segments.astype(jnp.float32)
    seg_wire = seg_values.astype(jnp.bfloat16)[None, :]
    lower = (queries[:half].reshape(half, head_count, HD), positions[:half], seg_values[:half])
    upper = (queries[half:].reshape(half, head_count, HD), positions[half:], seg_values[half:])
    groups = (lower, upper)
    start_state = (
        jnp.full((head_count, half), masked_score, jnp.float32),
        jnp.zeros((head_count, half), jnp.float32),
        jnp.zeros((head_count, half, HD), jnp.float32),
    )
    attend = functools.partial(attend_piece, groups=groups, head_count=head_count)
    states = attend(
        (start_state, start_state),
        (
            lax.all_gather(keys_vals, "seq", axis=1, tiled=True),
            lax.all_gather(seg_wire, "seq", axis=1, tiled=True),
        ),
        jnp.int32(0),
    )
    lower_out = finish(states[0], width)
    upper_out = finish(states[1], width)
    attended = jnp.concatenate([lower_out, upper_out], axis=0)
    partial_sums = jnp.dot(attended, w_out, preferred_element_type=jnp.float32)
    return lax.psum_scatter(partial_sums, "head", scatter_dimension=1, tiled=True).astype(
        jnp.bfloat16
    )


def solution(mesh):
    in_specs = (P("seq", "head"), P(), P(None, None, "head"), P("head", None), P("seq"))
    out_specs = P("seq", "head")
    return jax.shard_map(
        per_device, mesh=mesh, in_specs=in_specs, out_specs=out_specs, check_vma=False
    )
```

profile of v0, /device:TPU:2, one launch (start us, length us, event | category | flops | bytes accessed | tf_op | source)
XLA Modules:
  0.0 261.9 jit_solution(16025028984586071454)
XLA Ops:
  6.5 0.0 copy-start
  6.5 0.0 copy-start.3
  6.5 0.0 all-gather.4.cloned.1.call-start
  6.5 13.6 %all_gather.10 = bf16[256,1024]{1,0:T(8,128)(2,1)S(1)} all-gather(bf16[256,256]{1,0:T(8,128)(2,1)} %param.9), channel_id=1, replica_groups=mesh['seq'=64,'head'=4] {'head'}, dimensions={1}, use_global_device_ids=true | all-gather | bytes 655360 | tf_op jit(solution)/shard_map/all_gather | solution.py:65
  20.2 0.2 fusion.20
  20.4 1.7 copy.23
  22.1 1.3 fusion.37
  23.4 0.7 pad_maximum_fusion
  24.2 0.0 all-gather.4.cloned.1.call-update
  24.2 0.0 reduce-scatter.2.cloned.1.call-start
  24.2 0.0 copy-done.3
  24.3 46.5 %all-gather.1 = bf16[64,1,256]{2,1,0:T(2,128)(2,1)S(1)} all-gather(bf16[1,1,256]{2,1,0:T(2,128)(2,1)S(1)} %reshape.149), channel_id=2, replica_groups=mesh['seq'=64,'head'=4] {'seq'}, dimensions={0}, use_global_device_ids=true | all-gather | bytes 33280 | tf_op jit(solution)/shard_map/all_gather | solution.py:100
  70.8 0.1 convert_element_type.72
  70.8 0.0 copy-start.1
  70.9 0.7 slice.54
  71.5 0.7 slice_reduce_fusion.2
  73.6 0.7 slice_reduce_fusion.3
  76.9 48.2 %all-gather.4.cloned.1.call-done = bf16[2,16384,256]{2,1,0:T(8,128)(2,1)} async-done(((bf16[2,256,256]{2,1,0:T(8,128)(2,1)}), bf16[2,16384,256]{2,1,0:T(8,128)(2,1)}) %all-gather.4.cloned.1.call-update) | async-done | bytes 16777232 | tf_op jit(solution)/shard_map/all_gather | solution.py:99
  125.2 11.3 %fusion.35 = (bf16[1,16384,256]{2,1,0:T(8,128)(2,1)}, bf16[1,16384,256]{2,1,0:T(8,128)(2,1)}) fusion(bf16[2,16384,256]{2,1,0:T(8,128)(2,1)} %all-gather.4.cloned.1.call-done), kind=kLoop, calls=%fused_computation.55 | loop fusion | bytes 33554432 | tf_op jit(solution)/shard_map/slice | solution.py:18
  136.5 12.5 %reshape_squeeze.6 = bf16[16384,2,128]{2,1,0:T(2,128)(2,1)} reshape(bf16[1,16384,256]{2,1,0:T(8,128)(2,1)} %get-tuple-element.112) | data formatting | bytes 16777216 | tf_op jit(solution)/shard_map/reshape;squeeze | solution.py:17
  149.0 12.6 %reshape_squeeze.7 = bf16[16384,2,128]{2,1,0:T(2,128)(2,1)} reshape(bf16[1,16384,256]{2,1,0:T(8,128)(2,1)} %get-tuple-element.111) | data formatting | bytes 16777216 | tf_op jit(solution)/shard_map/reshape;squeeze | solution.py:18
  161.6 0.0 copy-done.1
  161.6 33.0 %conditional.2 = (f32[2,128]{1,0:T(2,128)S(1)}, f32[2,128,128]{1,2,0:T(8,128)S(1)}) conditional(s32[]{:T(128)} %convert_element_type.58, () %tuple.21, (s32[16384]{0:T(1024)S(1)}, s32[128]{0:T(128)S(1)}, f32[16384]{0:T(1024)S(1)}, f32[128]{0:T(128)S(1)}, bf16[256,256]{1,0:T(8,128)(2,1)S(1)}, /*index=5*/bf16[16384,2,128]{2,1,0:T(2,128)(2,1)}, ...), branch_computations={%region_3.0_spmd, %region_4.7_spmd} | conditional | flops 2187329280 | bytes 76487728 | solution.py:54
  161.6 0.0 copy-start.2
  161.6 0.6 copy-done.2
  162.2 2.5 compare_and_fusion
  164.7 0.1 copy.24
  164.9 10.7 %fusion.33 = (f32[2,128]{1,0:T(2,128)S(1)}, f32[2,128,16384]{2,1,0:T(8,128)}) fusion(bf16[128,2,128]{0,2,1:T(8,128)(2,1)S(1)} %bitcast.24, bf16[16384,2,128]{2,1,0:T(2,128)(2,1)} %get-tuple-element.92, pred[128,16384]{1,0:T(8,128)(4,1)S(1)} %compare_and_fusion), kind=kOutput, calls=%fused_computation.53 | convolution fusion | flops 1082130176 | bytes 27329536 | tf_op jit(solution)/shard_map/cond/branch_1_fun/qhd,khd->hqk/dot_general | solution.py:32
  175.5 11.1 %fusion.2 = f32[2,128,128]{1,2,0:T(8,128)S(1)} fusion(f32[2,128,16384]{2,1,0:T(8,128)} %get-tuple-element.108, bf16[16384,2,128]{2,1,0:T(2,128)(2,1)} %get-tuple-element.93, f32[2,128]{1,0:T(2,128)S(1)} %broadcast_maximum_fusion, pred[128,16384]{1,0:T(8,128)(4,1)S(1)} %compare_and_fusion), kind=kOutput, calls=%fused_computation.4 | convolution fusion | flops 1086324736 | bytes 27395072 | tf_op jit(solution)/shard_map/cond | solution.py:54
  186.6 8.0 %fusion.1 = f32[2,128]{1,0:T(2,128)S(1)} fusion(f32[2,128,16384]{2,1,0:T(8,128)} %get-tuple-element.108, f32[2,128]{1,0:T(2,128)S(1)} %broadcast_maximum_fusion, pred[128,16384]{1,0:T(8,128)(4,1)S(1)} %compare_and_fusion), kind=kLoop, calls=%fused_computation.3 | loop fusion | flops 12582656 | bytes 18876416 | tf_op jit(solution)/shard_map/cond/branch_1_fun/reduce_sum | solution.py:42
  194.7 32.6 %conditional.3 = (f32[2,128]{1,0:T(2,128)S(1)}, f32[2,128,128]{1,2,0:T(8,128)S(1)}) conditional(s32[]{:T(128)} %convert_element_type.66, () %tuple.23, (s32[16384]{0:T(1024)S(1)}, s32[128]{0:T(128)S(1)}, f32[16384]{0:T(1024)}, f32[128]{0:T(128)S(1)}, bf16[256,256]{1,0:T(8,128)(2,1)S(1)}, /*index=5*/bf16[16384,2,128]{2,1,0:T(2,128)(2,1)}, ...), branch_computations={%region_9.10_spmd, %region_10.13_spmd} | conditional | flops 2187329280 | bytes 76225552 | solution.py:54
  194.9 2.5 compare_and_fusion.1
  197.4 0.1 copy.28
  197.5 10.7 %fusion.34 = (f32[2,128]{1,0:T(2,128)S(1)}, f32[2,128,16384]{2,1,0:T(8,128)}) fusion(bf16[128,2,128]{0,2,1:T(8,128)(2,1)S(1)} %bitcast.25, bf16[16384,2,128]{2,1,0:T(2,128)(2,1)} %get-tuple-element.99, pred[128,16384]{1,0:T(8,128)(4,1)S(1)} %compare_and_fusion.1), kind=kOutput, calls=%fused_computation.54 | convolution fusion | flops 1082130176 | bytes 27329536 | tf_op jit(solution)/shard_map/cond/branch_1_fun/qhd,khd->hqk/dot_general | solution.py:32
  208.2 11.1 %fusion.12 = f32[2,128,128]{1,2,0:T(8,128)S(1)} fusion(f32[2,128,16384]{2,1,0:T(8,128)} %get-tuple-element.110, bf16[16384,2,128]{2,1,0:T(2,128)(2,1)} %get-tuple-element.100, f32[2,128]{1,0:T(2,128)S(1)} %broadcast_maximum_fusion.1, pred[128,16384]{1,0:T(8,128)(4,1)S(1)} %compare_and_fusion.1), kind=kOutput, calls=%fused_computation.17 | convolution fusion | flops 1086324736 | bytes 27395072 | tf_op jit(solution)/shard_map/cond | solution.py:54
  219.2 8.0 %fusion.11 = f32[2,128]{1,0:T(2,128)S(1)} fusion(f32[2,128,16384]{2,1,0:T(8,128)} %get-tuple-element.110, f32[2,128]{1,0:T(2,128)S(1)} %broadcast_maximum_fusion.1, pred[128,16384]{1,0:T(8,128)(4,1)S(1)} %compare_and_fusion.1), kind=kLoop, calls=%fused_computation.16 | loop fusion | flops 12582656 | bytes 18876416 | tf_op jit(solution)/shard_map/cond/branch_1_fun/reduce_sum | solution.py:42
  227.3 0.0 copy-done
  227.3 1.3 fusion.28
  228.6 0.0 reduce-scatter.2.cloned.1.call-update
  228.6 24.8 %reduce-scatter.2.cloned.1.call-done = f32[256,256]{1,0:T(8,128)} async-done(((f32[256,1024]{1,0:T(8,128)}), f32[256,256]{1,0:T(8,128)}) %reduce-scatter.2.cloned.1.call-update) | async-done | bytes 262160 | tf_op jit(solution)/shard_map/reduce_scatter | solution.py:108
  253.4 1.6 convert_element_type.70
  (14 shorter events, 0.2 us)
Async XLA Ops:
  6.5 220.8 %copy-start = (bf16[256,1024]{1,0:T(8,128)(2,1)S(1)}, bf16[256,1024]{1,0:T(8,128)(2,1)}, u32[]{:S(2)}) copy-start(bf16[256,1024]{1,0:T(8,128)(2,1)} %param.12) | copy-start | bytes 1572868
  6.5 17.7 %copy-start.3 = (s32[256]{0:T(256)S(1)}, s32[256]{0:T(256)}, u32[]{:S(2)}) copy-start(s32[256]{0:T(256)} %param.13) | copy-start | bytes 3076
  6.5 118.6 %all-gather.4.cloned.1.call-start = ((), (), s32[]{:S(2)}) async-start(), calls=%async_computation.1 | async-start | bytes 17039360 | tf_op jit(solution)/shard_map/all_gather | solution.py:99
  24.2 229.2 %reduce-scatter.2.cloned.1.call-start = ((), (), s32[]{:S(2)}) async-start(), calls=%async_computation.2 | async-start | bytes 1310720 | tf_op jit(solution)/shard_map/reduce_scatter | solution.py:108
  70.8 90.7 %copy-start.1 = (f32[64,1,256]{2,1,0:T(1,128)}, f32[64,1,256]{2,1,0:T(1,128)S(1)}, u32[]{:S(2)}) copy-start(f32[64,1,256]{2,1,0:T(1,128)S(1)} %convert_element_type.72) | copy-start | bytes 196612
  161.6 0.6 copy-start.2
Sparse Core Ops, SparseCore 0:
  24.3 100.7 all-gather.3
  228.8 24.6 reduce-scatter.1
where the time goes:
time: 263 us; the launch traced here: 262 us
  waiting for transfers between devices  73 us (28%)
  blocking collectives  60.1 us (23%)
  matrix products  46 us (17%)
  local copies, waits for them, and re-layouts  39.6 us (15%)
  other arithmetic  25.2 us (10%)
  between operations  17.5 us (7%)
    all_gather x1, waiting for transfers between devices, per_device(): lax.all_gather(keys_vals, 'seq', axis=1, tiled=True)  48.2 us
    all_gather x1, blocking collectives, per_device(): lax.all_gather(seg_wire, 'seq', axis=1, tiled=True)  46.5 us
    reduce_scatter x1, waiting for transfers between devices, per_device(): lax.psum_scatter(partial_sums, 'head', scatter_dimension=1, tiled=True)  24.8 us
    cond x2, matrix products, attend_piece(): updated.append(lax.cond(needed, update, lambda current: current, state))  22.1 us
    dot_general x2, matrix products, update(): jnp.einsum('qhd,khd->hqk', group_queries, key_rows, preferred_element_typ...  21.3 us
    reduce_sum x2, other arithmetic, update(): new_total = jnp.sum(weights, axis=2)  16 us
    all_gather x1, blocking collectives, per_device(): whole = lax.all_gather(face_rows, 'head', axis=1, tiled=True)  13.6 us
    another operation x1, local copies, waits for them, and re-layouts, attend_piece(): value_rows = keys_vals[1].reshape(key_count, head_count, head_size)  12.6 us
  transfers between devices with their start and end apart: 2, of which 2 were waited for; matrix products, arithmetic and copies ran while one was open for 1% of the time, Pallas kernels for 0%

commit v1 on v0

--- a/solution.py
+++ b/solution.py
@@ -8,6 +8,13 @@
 HD = 128
 epsilon = 1e-05
 masked_score = -1e30
+
+
+def exchange_gather(x, axis, dim):
+    devices = lax.axis_size(axis)
+    tiles = jnp.stack([x for _ in range(devices)])
+    tiles = lax.all_to_all(tiles, axis, split_axis=0, concat_axis=0)
+    return jnp.concatenate(tiles, axis=dim)
 
 
 def attend_piece(states, piece, start, groups, head_count):
@@ -95,10 +102,7 @@
     attend = functools.partial(attend_piece, groups=groups, head_count=head_count)
     states = attend(
         (start_state, start_state),
-        (
-            lax.all_gather(keys_vals, "seq", axis=1, tiled=True),
-            lax.all_gather(seg_wire, "seq", axis=1, tiled=True),
-        ),
+        (exchange_gather(keys_vals, "seq", 1), lax.all_gather(seg_wire, "seq", axis=1, tiled=True)),
         jnp.int32(0),
     )
     lower_out = finish(states[0], width)

time: 263 us -> 612 us (2.33)
  blocking collectives: 60.1 us -> 412 us
  waiting for transfers between devices: 73 us -> 25.2 us
  local copies, waits for them, and re-layouts: 39.6 us -> 70.6 us
  starting transfers between devices: 0.04 us -> 12.4 us
    all_gather x1, blocking collectives: 46.5 us -> 398 us  [per_device(): lax.all_gather(seg_wire, 'seq', axis=1, tiled=True)]
    all_gather x1 -> x0, waiting for transfers between devices: 48.2 us -> none  [per_device(): lax.all_gather(keys_vals, 'seq', axis=1, tiled=True)]
    all_to_all x0 -> x1, starting transfers between devices: none -> 12.3 us  [exchange_gather(): tiles = lax.all_to_all(tiles, axis, split_axis=0, concat_axis=0)]
    slice x1 -> x2, local copies, waits for them, and re-layouts: 11.3 us -> 23 us  [attend_piece(): value_rows = keys_vals[1].reshape(key_count, head_count, head_size)]
    slice x0 -> x1, local copies, waits for them, and re-layouts: none -> 11.4 us  [attend_piece(): key_rows = keys_vals[0].reshape(key_count, head_count, head_size)]
  transfers between devices with their start and end apart: 2 -> 2, of which waited for: 2 -> 1; matrix products, arithmetic and copies ran while one was open for 1% -> 0% of each run, Pallas kernels for 0% -> 0%
where the time goes in v1:
time: 612 us; the launch traced here: 611 us
  blocking collectives  412 us (67%)
  local copies, waits for them, and re-layouts  70.6 us (12%)
  matrix products  48.6 us (8%)
  waiting for transfers between devices  25.2 us (4%)
  other arithmetic  24.5 us (4%)
  between operations  17.5 us (3%)
  starting transfers between devices  12.4 us (2%)
    all_gather x1, blocking collectives, per_device(): lax.all_gather(seg_wire, 'seq', axis=1, tiled=True)  398 us
    reduce_scatter x1, waiting for transfers between devices, per_device(): lax.psum_scatter(partial_sums, 'head', scatter_dimension=1, tiled=True)  25.1 us
    dot_general x2, matrix products, update(): jnp.einsum('qhd,khd->hqk', group_queries, key_rows, preferred_element_typ...  25 us
    slice x2, local copies, waits for them, and re-layouts, attend_piece(): value_rows = keys_vals[1].reshape(key_count, head_count, head_size)  23 us
    cond x2, matrix products, attend_piece(): updated.append(lax.cond(needed, update, lambda current: current, state))  21 us
    reduce_sum x2, other arithmetic, update(): new_total = jnp.sum(weights, axis=2)  16 us
    all_gather x1, blocking collectives, per_device(): whole = lax.all_gather(face_rows, 'head', axis=1, tiled=True)  13.6 us
    another operation x1, local copies, waits for them, and re-layouts, attend_piece(): value_rows = keys_vals[1].reshape(key_count, head_count, head_size)  13.5 us
  transfers between devices with their start and end apart: 2, of which 1 were waited for; matrix products, arithmetic and copies ran while one was open for 0% of the time, Pallas kernels for 0%

profile of v1, /device:TPU:2, one launch (start us, length us, event | category | flops | bytes accessed | tf_op | source)
XLA Modules:
  0.0 611.1 jit_solution(3723414596709580286)
XLA Ops:
  6.5 0.0 copy-start
  6.5 13.6 %all_gather.7 = bf16[256,1024]{1,0:T(8,128)(2,1)S(1)} all-gather(bf16[256,256]{1,0:T(8,128)(2,1)} %param.9), channel_id=1, replica_groups=mesh['seq'=64,'head'=4] {'head'}, dimensions={1}, use_global_device_ids=true | all-gather | bytes 655360 | tf_op jit(solution)/shard_map/all_gather | solution.py:72
  20.2 0.2 fusion.16
  20.4 1.7 copy.20
  22.1 1.3 fusion.33
  23.5 0.1 copy.21
  23.6 6.0 stack.11
  29.6 0.0 copy-start.3
  29.6 12.3 %all-to-all-start = ((bf16[64,2,256,256]{2,3,1,0:T(8,128)(2,1)}), bf16[64,2,256,256]{2,3,1,0:T(8,128)(2,1)}, u32[]{:S(2)}, u32[]{:S(2)}) async-start(bf16[64,2,256,256]{2,3,1,0:T(8,128)(2,1)} %stack.11), calls=%async_computation | async-start | bytes 33554432 | tf_op jit(solution)/shard_map/all_to_all | solution.py:16
  41.9 0.0 reduce-scatter.2.cloned.1.call-start
  42.0 0.0 copy-done.3
  42.0 398.2 %all-gather.1 = bf16[64,1,256]{2,1,0:T(2,128)(2,1)S(1)} all-gather(bf16[1,1,256]{2,1,0:T(2,128)(2,1)S(1)} %reshape.169), channel_id=2, replica_groups=mesh['seq'=64,'head'=4] {'seq'}, dimensions={0}, use_global_device_ids=true | all-gather | bytes 33280 | tf_op jit(solution)/shard_map/all_gather | solution.py:105
  440.2 0.1 convert_element_type.74
  440.3 0.0 copy-start.1
  440.3 0.6 slice.56
  440.9 0.7 slice_reduce_fusion.2
  442.9 0.7 slice_reduce_fusion.3
  446.3 0.0 all-to-all-done
  446.3 11.6 %fusion.31 = (bf16[1,64,256,256]{2,3,0,1:T(8,128)(2,1)}, bf16[1,64,256,256]{2,3,0,1:T(8,128)(2,1)}) fusion(bf16[2,64,256,256]{2,3,0,1:T(8,128)(2,1)} %bitcast.8), kind=kLoop, calls=%fused_computation.51 | loop fusion | bytes 33554432 | tf_op jit(solution)/shard_map/slice | solution.py:25
  457.9 11.4 %copy.22 = bf16[1,64,256,256]{2,1,3,0:T(8,128)(2,1)} copy(bf16[1,64,256,256]{2,3,0,1:T(8,128)(2,1)} %get-tuple-element.98) | data formatting | bytes 16777216 | tf_op jit(solution)/shard_map/slice | solution.py:24
  469.3 13.5 %reshape_squeeze.6 = bf16[16384,2,128]{0,2,1:T(8,128)(2,1)} reshape(bf16[1,64,256,256]{2,1,3,0:T(8,128)(2,1)} %copy.22) | data formatting | bytes 16777216 | tf_op jit(solution)/shard_map/reshape;squeeze | solution.py:24
  482.7 11.4 %copy.23 = bf16[1,64,256,256]{2,1,3,0:T(8,128)(2,1)} copy(bf16[1,64,256,256]{2,3,0,1:T(8,128)(2,1)} %get-tuple-element.97) | data formatting | bytes 16777216 | tf_op jit(solution)/shard_map/slice | solution.py:25
  494.1 13.5 %reshape_squeeze.7 = bf16[16384,2,128]{0,2,1:T(8,128)(2,1)} reshape(bf16[1,64,256,256]{2,1,3,0:T(8,128)(2,1)} %copy.23) | data formatting | bytes 16777216 | tf_op jit(solution)/shard_map/reshape;squeeze | solution.py:25
  507.6 0.0 copy-done.1
  507.6 34.5 %conditional.2 = (f32[2,128]{1,0:T(2,128)S(1)}, f32[2,128,128]{1,2,0:T(8,128)S(1)}) conditional(s32[]{:T(128)} %convert_element_type.60, () %tuple.21, (s32[16384]{0:T(1024)S(1)}, s32[128]{0:T(128)S(1)}, f32[16384]{0:T(1024)S(1)}, f32[128]{0:T(128)S(1)}, bf16[256,256]{1,0:T(8,128)(2,1)S(1)}, /*index=5*/bf16[16384,2,128]{0,2,1:T(8,128)(2,1)}, ...), branch_computations={%region_3.0_spmd, %region_4.7_spmd} | conditional | flops 2187329280 | bytes 76487728 | solution.py:61
  507.8 0.0 copy-start.2
  507.9 0.6 copy-done.2
  508.5 2.5 compare_and_fusion
  511.0 0.1 copy.24
  511.1 12.5 %fusion.29 = (f32[2,128]{1,0:T(2,128)S(1)}, f32[2,128,16384]{2,1,0:T(8,128)}) fusion(bf16[128,2,128]{0,2,1:T(8,128)(2,1)S(1)} %bitcast.37, bf16[16384,2,128]{0,2,1:T(8,128)(2,1)} %get-tuple-element.78, pred[128,16384]{1,0:T(8,128)(4,1)S(1)} %compare_and_fusion), kind=kOutput, calls=%fused_computation.49 | convolution fusion | flops 1082130176 | bytes 27329536 | tf_op jit(solution)/shard_map/cond/branch_1_fun/qhd,khd->hqk/dot_general | solution.py:39
  523.6 10.5 %fusion.2 = f32[2,128,128]{1,2,0:T(8,128)S(1)} fusion(bf16[16384,2,128]{0,2,1:T(8,128)(2,1)} %get-tuple-element.79, f32[2,128,16384]{2,1,0:T(8,128)} %get-tuple-element.94, f32[2,128]{1,0:T(2,128)S(1)} %broadcast_maximum_fusion, pred[128,16384]{1,0:T(8,128)(4,1)S(1)} %compare_and_fusion), kind=kOutput, calls=%fused_computation.4 | convolution fusion | flops 1086324736 | bytes 27395072 | tf_op jit(solution)/shard_map/cond | solution.py:61
  534.1 8.0 %fusion.1 = f32[2,128]{1,0:T(2,128)S(1)} fusion(f32[2,128,16384]{2,1,0:T(8,128)} %get-tuple-element.94, f32[2,128]{1,0:T(2,128)S(1)} %broadcast_maximum_fusion, pred[128,16384]{1,0:T(8,128)(4,1)S(1)} %compare_and_fusion), kind=kLoop, calls=%fused_computation.3 | loop fusion | flops 12582656 | bytes 18876416 | tf_op jit(solution)/shard_map/cond/branch_1_fun/reduce_sum | solution.py:49
  542.2 33.9 %conditional.3 = (f32[2,128]{1,0:T(2,128)S(1)}, f32[2,128,128]{1,2,0:T(8,128)S(1)}) conditional(s32[]{:T(128)} %convert_element_type.68, () %tuple.23, (s32[16384]{0:T(1024)S(1)}, s32[128]{0:T(128)S(1)}, f32[16384]{0:T(1024)}, f32[128]{0:T(128)S(1)}, bf16[256,256]{1,0:T(8,128)(2,1)S(1)}, /*index=5*/bf16[16384,2,128]{0,2,1:T(8,128)(2,1)}, ...), branch_computations={%region_9.10_spmd, %region_10.13_spmd} | conditional | flops 2187329280 | bytes 76225552 | solution.py:61
  542.4 2.5 compare_and_fusion.1
  545.0 0.1 copy.28
  545.1 12.5 %fusion.30 = (f32[2,128]{1,0:T(2,128)S(1)}, f32[2,128,16384]{2,1,0:T(8,128)}) fusion(bf16[128,2,128]{0,2,1:T(8,128)(2,1)S(1)} %bitcast.38, bf16[16384,2,128]{0,2,1:T(8,128)(2,1)} %get-tuple-element.85, pred[128,16384]{1,0:T(8,128)(4,1)S(1)} %compare_and_fusion.1), kind=kOutput, calls=%fused_computation.50 | convolution fusion | flops 1082130176 | bytes 27329536 | tf_op jit(solution)/shard_map/cond/branch_1_fun/qhd,khd->hqk/dot_general | solution.py:39
  557.6 10.5 %fusion.10 = f32[2,128,128]{1,2,0:T(8,128)S(1)} fusion(bf16[16384,2,128]{0,2,1:T(8,128)(2,1)} %get-tuple-element.86, f32[2,128,16384]{2,1,0:T(8,128)} %get-tuple-element.96, f32[2,128]{1,0:T(2,128)S(1)} %broadcast_maximum_fusion.1, pred[128,16384]{1,0:T(8,128)(4,1)S(1)} %compare_and_fusion.1), kind=kOutput, calls=%fused_computation.15 | convolution fusion | flops 1086324736 | bytes 27395072 | tf_op jit(solution)/shard_map/cond | solution.py:61
  568.1 8.0 %fusion.9 = f32[2,128]{1,0:T(2,128)S(1)} fusion(f32[2,128,16384]{2,1,0:T(8,128)} %get-tuple-element.96, f32[2,128]{1,0:T(2,128)S(1)} %broadcast_maximum_fusion.1, pred[128,16384]{1,0:T(8,128)(4,1)S(1)} %compare_and_fusion.1), kind=kLoop, calls=%fused_computation.14 | loop fusion | flops 12582656 | bytes 18876416 | tf_op jit(solution)/shard_map/cond/branch_1_fun/reduce_sum | solution.py:49
  576.1 0.0 copy-done
  576.1 1.3 fusion.24
  577.5 0.0 reduce-scatter.2.cloned.1.call-update
  577.5 25.1 %reduce-scatter.2.cloned.1.call-done = f32[256,256]{1,0:T(8,128)} async-done(((f32[256,1024]{1,0:T(8,128)}), f32[256,256]{1,0:T(8,128)}) %reduce-scatter.2.cloned.1.call-update) | async-done | bytes 262160 | tf_op jit(solution)/shard_map/reduce_scatter | solution.py:112
  602.6 1.6 convert_element_type.72
  (15 shorter events, 0.2 us)
Async XLA Ops:
  6.5 569.6 %copy-start = (bf16[256,1024]{1,0:T(8,128)(2,1)S(1)}, bf16[256,1024]{1,0:T(8,128)(2,1)}, u32[]{:S(2)}) copy-start(bf16[256,1024]{1,0:T(8,128)(2,1)} %param.12) | copy-start | bytes 1572868
  29.6 12.4 %copy-start.3 = (s32[256]{0:T(256)S(1)}, s32[256]{0:T(256)}, u32[]{:S(2)}) copy-start(s32[256]{0:T(256)} %param.13) | copy-start | bytes 3076
  29.6 416.7 %all-to-all-start = ((bf16[64,2,256,256]{2,3,1,0:T(8,128)(2,1)}), bf16[64,2,256,256]{2,3,1,0:T(8,128)(2,1)}, u32[]{:S(2)}, u32[]{:S(2)}) async-start(bf16[64,2,256,256]{2,3,1,0:T(8,128)(2,1)} %stack.11), calls=%async_computation | async-start | bytes 33554432 | tf_op jit(solution)/shard_map/all_to_all | solution.py:16
  41.9 560.7 %reduce-scatter.2.cloned.1.call-start = ((), (), s32[]{:S(2)}) async-start(), calls=%async_computation.2 | async-start | bytes 1310720 | tf_op jit(solution)/shard_map/reduce_scatter | solution.py:112
  440.3 67.3 %copy-start.1 = (f32[64,1,256]{2,1,0:T(1,128)}, f32[64,1,256]{2,1,0:T(1,128)S(1)}, u32[]{:S(2)}) copy-start(f32[64,1,256]{2,1,0:T(1,128)S(1)} %convert_element_type.74) | copy-start | bytes 196612
  507.8 0.6 copy-start.2
Sparse Core Ops, SparseCore 0:
  577.6 24.9 reduce-scatter.1
